TPU v7x, 512 devices: a whole 4x4x16 slice. The times are simulated.
512 devices in a mesh: grp: 16 (over y, x_hi, core), seq: 32 (over z, x_lo).
Axes of the slice: x: 4 (x_hi: 2, x_lo: 2; x = x_hi * 2 + x_lo), y: 4, z: 16, core: 2. Of those that a mesh axis runs over, the one named last changes fastest.
Arguments:
- tokens: bfloat16 [16, 4096, 1024], P('grp', 'seq'), may hold values from -40 to 40
- queries: bfloat16 [16, 4096, 512], P('grp', 'seq'), may hold values from -8 to 8
- keys: bfloat16 [16, 4096, 512], P('grp', 'seq'), may hold values from -8 to 8
- values: bfloat16 [16, 4096, 512], P('grp', 'seq'), may hold values from -6 to 6
- attn_mask: int32 [16, 32, 32], P('grp', 'seq'), may hold values from 0 to 1, as said below
- out_proj: bfloat16 [512, 1024], replicated, may hold values from -0.25 to 0.25
- norm_gain_vector: float32 [1024], replicated, may hold values from 0.5 to 1.5
- w1_packed: bfloat16 [32, 2, 128, 128], P('grp'), may hold values from -0.375 to 0.375
- w1_rows: int32 [32, 2], replicated, may hold values from 0 to 7, as said below
- w2_packed: bfloat16 [32, 2, 128, 128], P('grp'), may hold values from -0.1875 to 0.1875
- w2_cols: int32 [32, 2], replicated, may hold values from 0 to 7, as said below
- grad_out: bfloat16 [16, 4096, 1024], P('grp', 'seq'), may hold values from -6 to 6
Outputs:
- output: bfloat16 [16, 4096, 1024], P('grp', 'seq')
- grad_tokens: bfloat16 [16, 4096, 1024], P('grp', 'seq')
Inputs may be any that keep to these rules, and one draw needn't show every extreme that they name: attn_mask[s, i, i] is 1 for every sheet s and block i. `w1_rows`: the 2 entries of a row are distinct. `w2_cols`: the 2 entries of a row are distinct.
All inputs are finite; a program needn't handle non-finite values.
Results may differ from a plain program's by a relative error of at most 0.0035.
The roundings to bfloat16 on the way count: a program that leaves them out, or rounds other values in their place, can miss the bound.
Values may be sent and summed in bfloat16 or wider, within the bound.
A program may use at most 64 MiB of HBM per device.

v0:
```python
import jax
import jax.numpy as jnp
from jax import lax
from jax.sharding import PartitionSpec as P

D = 1024
HD = 64
HEADS = 8
BLK = 128


def gelu_slope(pre):
    return (
        0.5 * (1.0 + jax.scipy.special.erf(pre * 0.7071067811865476))
        + pre * jnp.exp(-0.5 * pre * pre) * 0.3989422804014327
    )


def expand_mask(mask):
    rows_blk, cols_blk = mask.shape
    wide = jnp.broadcast_to(mask[:, None, :, None], (rows_blk, BLK, cols_blk, BLK))
    return wide.reshape(rows_blk * BLK, cols_blk * BLK) > 0


def split_heads(array):
    return array.reshape(array.shape[0], HEADS, HD).transpose(1, 0, 2)


def join_heads(array):
    return array.transpose(1, 0, 2).reshape(array.shape[1], HEADS * HD)


def attend_forward(query, key_rows, value_rows, allowed):
    scale = HD ** (-0.5)

    def one_head(args):
        q_head, k_head, v_head = args
        scores = jnp.dot(q_head, k_head.T, preferred_element_type=jnp.float32) * scale
        scores = jnp.where(allowed, scores, -jnp.inf)
        top = jnp.max(scores, axis=1, keepdims=True)
        weight = jnp.exp(scores - top)
        total = jnp.sum(weight, axis=1, keepdims=True)
        prob = (weight / total).astype(jnp.bfloat16)
        return jnp.dot(prob, v_head, preferred_element_type=jnp.float32)

    heads_out = lax.map(
        one_head, (split_heads(query), split_heads(key_rows), split_heads(value_rows))
    )
    return join_heads(heads_out).astype(jnp.bfloat16)


def layer_norm_forward(hidden_state, gain_vector):
    mean_row = jnp.mean(hidden_state, axis=1, keepdims=True)
    mean_removed = hidden_state - mean_row
    reciprocal_deviation = lax.rsqrt(
        jnp.mean(mean_removed * mean_removed, axis=1, keepdims=True) + 1e-06
    )
    unit_rows = mean_removed * reciprocal_deviation
    return (unit_rows, reciprocal_deviation, (unit_rows * gain_vector).astype(jnp.bfloat16))


def layer_norm_backward(
    normed_gradient, gain_vector, unit_rows, reciprocal_deviation, gradient_rows
):
    unit_gradient = normed_gradient * gain_vector
    inner_product = (
        unit_gradient
        - jnp.mean(unit_gradient, axis=1, keepdims=True)
        - unit_rows * jnp.mean(unit_gradient * unit_rows, axis=1, keepdims=True)
    )
    return (gradient_rows.astype(jnp.float32) + reciprocal_deviation * inner_product).astype(
        jnp.bfloat16
    )


def panel_terms(first_blocks, second_blocks, row_table, col_table, normed_rows, gradient_rows):
    tok_rows = normed_rows.shape[0]
    width_blocks = D // BLK
    block_ids = jnp.arange(width_blocks, dtype=jnp.int32)[None, None, :]
    row_place = (row_table[:, :, None] == block_ids).astype(jnp.float32)
    col_place = (col_table[:, :, None] == block_ids).astype(jnp.float32)
    normed_sel = jnp.take(normed_rows.reshape(tok_rows, width_blocks, BLK), row_table, axis=1)
    pre = jnp.einsum("tcnk,cnkj->tcj", normed_sel, first_blocks, preferred_element_type=jnp.float32)
    act = jax.nn.gelu(pre, approximate=False).astype(jnp.bfloat16)
    forward_part = jnp.einsum(
        "tck,cnkj->tcnj", act, second_blocks, preferred_element_type=jnp.float32
    )
    mlp_part = jnp.einsum(
        "tcnj,cnb->tbj", forward_part, col_place, precision=lax.Precision.HIGHEST
    ).reshape(tok_rows, D)
    grad_sel = jnp.take(gradient_rows.reshape(tok_rows, width_blocks, BLK), col_table, axis=1)
    dact = jnp.einsum("tcnj,cnkj->tck", grad_sel, second_blocks, preferred_element_type=jnp.float32)
    dpre = (dact * gelu_slope(pre)).astype(jnp.bfloat16)
    back_part = jnp.einsum("tcj,cnkj->tcnk", dpre, first_blocks, preferred_element_type=jnp.float32)
    dnormed_part = jnp.einsum(
        "tcnk,cnb->tbk", back_part, row_place, precision=lax.Precision.HIGHEST
    ).reshape(tok_rows, D)
    return (mlp_part, dnormed_part)


def body(
    tokens,
    queries,
    keys,
    values,
    attn_mask,
    out_proj,
    norm_gain_vector,
    w1_packed,
    w1_rows,
    w2_packed,
    w2_cols,
    grad_out,
):
    rows_in = tokens[0]
    query = queries[0]
    gradient_rows = grad_out[0]
    allowed = expand_mask(attn_mask[0])
    key_rows, value_rows = (
        lax.all_gather(keys[0], "seq", axis=0, tiled=True),
        lax.all_gather(values[0], "seq", axis=0, tiled=True),
    )
    attn = attend_forward(query, key_rows, value_rows, allowed)
    hidden_state = rows_in.astype(jnp.float32) + jnp.dot(
        attn, out_proj, preferred_element_type=jnp.float32
    )
    unit_rows, reciprocal_deviation, normed_rows = layer_norm_forward(
        hidden_state, norm_gain_vector
    )
    first_all, second_all = (
        lax.all_gather(w1_packed, "grp", axis=0, tiled=True),
        lax.all_gather(w2_packed, "grp", axis=0, tiled=True),
    )
    mlp, normed_gradient = panel_terms(
        first_all, second_all, w1_rows, w2_cols, normed_rows, gradient_rows
    )
    result = (hidden_state + mlp).astype(jnp.bfloat16)
    incoming_gradient_rows = layer_norm_backward(
        normed_gradient, norm_gain_vector, unit_rows, reciprocal_deviation, gradient_rows
    )
    return (result[None], incoming_gradient_rows[None])


def solution(mesh):
    return jax.shard_map(
        body,
        mesh=mesh,
        in_specs=(
            P("grp", "seq", None),
            P("grp", "seq", None),
            P("grp", "seq", None),
            P("grp", "seq", None),
            P("grp", "seq", None),
            P(),
            P(),
            P("grp", None, None, None),
            P(),
            P("grp", None, None, None),
            P(),
            P("grp", "seq", None),
        ),
        out_specs=(P("grp", "seq", None), P("grp", "seq", None)),
        check_vma=False,
    )
```

profile of v0, /device:TPU:1, one launch (start us, length us, event | category | flops | bytes accessed | tf_op | source)
XLA Modules:
  0.0 497.4 jit_solution(4746874300129246282)
XLA Ops:
  7.2 1.7 copy.46
  9.0 1.7 copy.47
  16.9 1.1 copy.56
  18.5 2.1 gather_fusion.1
  20.6 133.6 %all-gather.11.cloned.1.call-done = bf16[1,4096,512]{1,2,0:T(8,128)(2,1)} async-done(((bf16[1,128,512]{1,2,0:T(8,128)(2,1)}), bf16[1,4096,512]{1,2,0:T(8,128)(2,1)}) %all-gather.11.cloned.1.call-update) | async-done | bytes 4194320 | tf_op jit(solution)/shard_map/all_gather | solution.py:120
  154.2 160.8 %all-gather.13.cloned.1.call-done = bf16[1,4096,512]{1,2,0:T(8,128)(2,1)} async-done(((bf16[1,128,512]{1,2,0:T(8,128)(2,1)}), bf16[1,4096,512]{1,2,0:T(8,128)(2,1)}) %all-gather.13.cloned.1.call-update) | async-done | bytes 4194320 | tf_op jit(solution)/shard_map/all_gather | solution.py:121
  315.1 29.5 %while.11 = (s32[]{:T(128)}, bf16[8,128,64]{1,2,0:T(8,128)(2,1)S(1)}, bf16[8,128,64]{1,2,0:T(8,128)(2,1)S(1)}, bf16[8,4096,64]{1,2,0:T(8,128)(2,1)}, bf16[8,4096...) while((s32[]{:T(128)}, bf16[8,128,64]{1,2,0:T(8,128)(2,1)S(1)}, ...), condition=%wide.region_3.4_spmd.clone, body=%wide.region_0.3_spmd.clone.sunk | while | flops 138411776 | bytes 7397965 | solution.py:46
  315.1 1.6 fusion.158
  317.1 1.6 fusion.160
  318.8 1.6 fusion.158
  320.8 1.6 fusion.160
  322.5 1.6 fusion.158
  324.5 1.6 fusion.160
  326.1 1.6 fusion.158
  328.2 1.6 fusion.160
  329.8 1.6 fusion.158
  331.9 1.6 fusion.160
  333.5 1.6 fusion.158
  335.5 1.6 fusion.160
  337.2 1.6 fusion.158
  339.2 1.6 fusion.160
  340.9 1.6 fusion.158
  342.9 1.6 fusion.160
  345.4 2.2 gather_fusion
  347.6 54.0 %all-gather.7.cloned.1.call-done = bf16[32,2,128,128]{3,2,1,0:T(8,128)(2,1)} async-done(((bf16[2,2,128,128]{3,2,1,0:T(8,128)(2,1)}), bf16[32,2,128,128]{3,2,1,0:T(8,128)(2,1)}) %all-gather.7.cloned.1.call-update) | async-done | bytes 2097168 | tf_op jit(solution)/shard_map/all_gather | solution.py:131
  401.6 4.3 fusion.32
  405.9 60.7 %all-gather.9.cloned.1.call-done = bf16[32,2,128,128]{3,2,1,0:T(8,128)(2,1)} async-done(((bf16[2,2,128,128]{3,2,1,0:T(8,128)(2,1)}), bf16[32,2,128,128]{3,2,1,0:T(8,128)(2,1)}) %all-gather.9.cloned.1.call-update) | async-done | bytes 2097168 | tf_op jit(solution)/shard_map/all_gather | solution.py:132
  466.6 7.2 %convolution_bitcast_fusion.1 = f32[128,32,2,128]{3,0,2,1:T(8,128)} fusion(bf16[32,2,128,128]{3,2,1,0:T(8,128)(2,1)} %all-gather.7.cloned.1.call-done, f32[32,128,128,1]{2,1,3,0:T(8,128)} %fusion.32, bf16[32,2,128,128]{3,2,1,0:T(8,128)(2,1)} %all-gather.9.cloned.1.call-done, bf16[32,2,128,128]{3,2,1,0:T(8,128)(2,1)} %bitcast.202, pred[32,2]{1,0:T(8,128)(4,1)S(1)} %copy.55), kind=kOutput, calls=%fused_computation.24 | convolution fusion | flops 543162368 | bytes 12582976 | tf_op jit(solution)/shard_map/tcj,cnkj->tcnk/dot_general | solution.py:94
  473.8 6.7 %fusion.96 = (f32[128]{0:T(128)S(1)}, f32[8,128,128,1]{2,0,3,1:T(8,128)S(1)}) fusion(f32[8,128]{1,0:T(8,128)S(1)} %bitcast.208, f32[128,32,2,128]{3,0,2,1:T(8,128)} %convolution_bitcast_fusion.1, s32[32,2]{0,1:T(2,128)S(1)} %copy-done.5), kind=kOutput, calls=%fused_computation.111 | convolution fusion | flops 100925824 | bytes 4723456 | tf_op jit(solution)/shard_map/tcnk,cnb->tbk/dot_general | solution.py:95
  480.8 5.1 %convolution_bitcast_fusion.2 = f32[128,32,2,128]{3,0,2,1:T(8,128)S(1)} fusion(bf16[32,2,128,128]{3,2,1,0:T(8,128)(2,1)S(1)} %copy-done.7, f32[32,128,128,1]{2,1,3,0:T(8,128)S(1)} %copy-done.1), kind=kOutput, calls=%fused_computation.25 | convolution fusion | flops 302514176 | bytes 8388608 | tf_op jit(solution)/shard_map/tck,cnkj->tcnj/dot_general | solution.py:85
  485.9 3.8 fusion.15
  489.8 1.1 fusion.99
  (56 shorter events, 11.3 us)
Async XLA Ops:
  7.2 337.4 %copy-start = (bf16[512,1024]{1,0:T(8,128)(2,1)S(1)}, bf16[512,1024]{1,0:T(8,128)(2,1)}, u32[]{:S(2)}) copy-start(bf16[512,1024]{1,0:T(8,128)(2,1)} %param.21) | copy-start | bytes 3145732
  7.2 147.1 %all-gather.11.cloned.1.call-start = ((), (), s32[]{:S(2)}) async-start(), calls=%async_computation.2 | async-start | bytes 4325376 | tf_op jit(solution)/shard_map/all_gather | solution.py:120
  9.0 306.1 %all-gather.13.cloned.1.call-start = ((), (), s32[]{:S(2)}) async-start(), calls=%async_computation.3 | async-start | bytes 4325376 | tf_op jit(solution)/shard_map/all_gather | solution.py:121
  10.7 390.8 %all-gather.7.cloned.1.call-start = ((), (), s32[]{:S(2)}) async-start(), calls=%async_computation | async-start | bytes 2228224 | tf_op jit(solution)/shard_map/all_gather | solution.py:131
  11.5 455.1 %all-gather.9.cloned.1.call-start = ((), (), s32[]{:S(2)}) async-start(), calls=%async_computation.1 | async-start | bytes 2228224 | tf_op jit(solution)/shard_map/all_gather | solution.py:132
  315.1 29.5 %copy-start.3 = (bf16[1,128,1024]{2,1,0:T(8,128)(2,1)S(1)}, bf16[1,128,1024]{2,1,0:T(8,128)(2,1)}, u32[]{:S(2)}) copy-start(bf16[1,128,1024]{2,1,0:T(8,128)(2,1)} %param.16) | copy-start | bytes 786436
  344.5 0.7 copy-start.4
  466.6 7.2 %copy-start.5 = (s32[32,2]{0,1:T(2,128)S(1)}, s32[32,2]{0,1:T(2,128)}, u32[]{:S(2)}) copy-start(s32[32,2]{0,1:T(2,128)} %param.24) | copy-start | bytes 772
  473.8 7.0 %copy-start.1 = (f32[32,128,128,1]{2,1,3,0:T(8,128)S(1)}, f32[32,128,128,1]{2,1,3,0:T(8,128)}, u32[]{:S(2)}) copy-start(f32[32,128,128,1]{2,1,3,0:T(8,128)} %fusion.32) | copy-start | bytes 6291460
  473.8 7.0 %copy-start.7 = (bf16[32,2,128,128]{3,2,1,0:T(8,128)(2,1)S(1)}, bf16[32,2,128,128]{3,2,1,0:T(8,128)(2,1)}, u32[]{:S(2)}) copy-start(bf16[32,2,128,128]{3,2,1,0:T(8,128)(2,1)} %all-gather.9.cloned.1.call-done) | copy-start | bytes 6291460
  480.8 5.2 %copy-start.6 = (s32[32,2]{0,1:T(2,128)S(1)}, s32[32,2]{0,1:T(2,128)}, u32[]{:S(2)}) copy-start(s32[32,2]{0,1:T(2,128)} %param.26) | copy-start | bytes 772
  485.9 3.8 copy-start.2
Sparse Core Ops, SparseCore 0:
  10.6 143.6 all-gather.10
  156.8 158.1 all-gather.12
  318.4 83.1 all-gather.6
  404.8 61.7 all-gather.8
where the time goes:
time: 498 us; the launch traced here: 497 us
  waiting for transfers between devices  410 us (82%)
  matrix products  53.3 us (11%)
  between operations  13.9 us (3%)
  local copies, waits for them, and re-layouts  10.8 us (2%)
  other arithmetic  8.65 us (2%)
    all_gather x1, waiting for transfers between devices, body(): lax.all_gather(values[0], 'seq', axis=0, tiled=True)  161 us
    all_gather x1, waiting for transfers between devices, body(): lax.all_gather(keys[0], 'seq', axis=0, tiled=True)  134 us
    all_gather x1, waiting for transfers between devices, body(): lax.all_gather(w2_packed, 'grp', axis=0, tiled=True)  60.7 us
    all_gather x1, waiting for transfers between devices, body(): lax.all_gather(w1_packed, 'grp', axis=0, tiled=True)  54 us
    dot_general x8, matrix products, one_head(): return jnp.dot(prob, v_head, preferred_element_type=jnp.float32)  13 us
    dot_general x8, matrix products, one_head(): jnp.dot(q_head, k_head.T, preferred_element_type=jnp.float32) * scale  12.7 us
  transfers between devices with their start and end apart: 4, of which 4 were waited for; matrix products, arithmetic and copies ran while one was open for 9% of the time, Pallas kernels for 0%

commit v1 on v0

--- a/solution.py
+++ b/solution.py
@@ -7,6 +7,19 @@
 HD = 64
 HEADS = 8
 BLK = 128
+
+
+def guide_groups(m, lane_axis):
+    all_values = jnp.concatenate(
+        lax.all_to_all(
+            jnp.stack([m for _ in range(lax.axis_size(lane_axis))]),
+            axis_name=lane_axis,
+            split_axis=0,
+            concat_axis=0,
+        ),
+        0,
+    )
+    return all_values
 
 
 def gelu_slope(pre):
@@ -118,7 +131,7 @@
     allowed = expand_mask(attn_mask[0])
     key_rows, value_rows = (
         lax.all_gather(keys[0], "seq", axis=0, tiled=True),
-        lax.all_gather(values[0], "seq", axis=0, tiled=True),
+        guide_groups(values[0], "seq"),
     )
     attn = attend_forward(query, key_rows, value_rows, allowed)
     hidden_state = rows_in.astype(jnp.float32) + jnp.dot(

time: 498 us -> 455 us (0.914)
  waiting for transfers between devices: 410 us -> 339 us
  starting transfers between devices: 0.16 us -> 17.3 us
  local copies, waits for them, and re-layouts: 10.8 us -> 24.6 us
    all_to_all x0 -> x1, waiting for transfers between devices: none -> 194 us  [guide_groups(): lax.all_to_all(jnp.stack([m for _ in range(lax.axis_size(lane_axis))]), a...]
    all_gather x1 -> x0, waiting for transfers between devices: 161 us -> none  [body(): lax.all_gather(values[0], 'seq', axis=0, tiled=True)]
    all_gather x1, waiting for transfers between devices: 134 us -> 40.1 us  [body(): lax.all_gather(keys[0], 'seq', axis=0, tiled=True)]
    all_to_all x0 -> x1, starting transfers between devices: none -> 17.2 us  [guide_groups(): lax.all_to_all(jnp.stack([m for _ in range(lax.axis_size(lane_axis))]), a...]
    another operation x0 -> x3, local copies, waits for them, and re-layouts: none -> 11.4 us  [the longest x1 7.38 us: split_heads(): return array.reshape(array.shape[0], HEADS, HD).transpose(1, 0, 2)]
    all_gather x1, waiting for transfers between devices: 54 us -> 42.7 us  [body(): lax.all_gather(w1_packed, 'grp', axis=0, tiled=True)]
    all_to_all x0 -> x1, local copies, waits for them, and re-layouts: none -> 6.9 us  [guide_groups(): lax.all_to_all(jnp.stack([m for _ in range(lax.axis_size(lane_axis))]), a...]
  transfers between devices with their start and end apart: 4 -> 4, of which waited for: 4 -> 4; matrix products, arithmetic and copies ran while one was open for 9% -> 12% of each run, Pallas kernels for 0% -> 0%
where the time goes in v1:
time: 455 us; the launch traced here: 453 us
  waiting for transfers between devices  339 us (75%)
  matrix products  53.4 us (12%)
  local copies, waits for them, and re-layouts  24.6 us (5%)
  starting transfers between devices  17.3 us (4%)
  between operations  14 us (3%)
  other arithmetic  5.28 us (1%)
    all_to_all x1, waiting for transfers between devices, guide_groups(): lax.all_to_all(jnp.stack([m for _ in range(lax.axis_size(lane_axis))]), a...  194 us
    all_gather x1, waiting for transfers between devices, body(): lax.all_gather(w2_packed, 'grp', axis=0, tiled=True)  60.9 us
    all_gather x1, waiting for transfers between devices, body(): lax.all_gather(w1_packed, 'grp', axis=0, tiled=True)  42.7 us
    all_gather x1, waiting for transfers between devices, body(): lax.all_gather(keys[0], 'seq', axis=0, tiled=True)  40.1 us
    all_to_all x1, starting transfers between devices, guide_groups(): lax.all_to_all(jnp.stack([m for _ in range(lax.axis_size(lane_axis))]), a...  17.2 us
    dot_general x8, matrix products, one_head(): return jnp.dot(prob, v_head, preferred_element_type=jnp.float32)  13 us
    dot_general x8, matrix products, one_head(): jnp.dot(q_head, k_head.T, preferred_element_type=jnp.float32) * scale  12.7 us
  transfers between devices with their start and end apart: 4, of which 4 were waited for; matrix products, arithmetic and copies ran while one was open for 12% of the time, Pallas kernels for 0%

profile of v1, /device:TPU:1, one launch (start us, length us, event | category | flops | bytes accessed | tf_op | source)
XLA Modules:
  0.0 453.4 jit_solution(1834974135162687152)
XLA Ops:
  8.3 2.9 stack.3
  11.2 17.2 %all-to-all-start = ((bf16[32,128,512]{1,2,0:T(8,128)(2,1)}), bf16[32,128,512]{1,2,0:T(8,128)(2,1)}, u32[]{:S(2)}, u32[]{:S(2)}) async-start(bf16[32,128,512]{1,2,0:T(8,128)(2,1)} %stack.3), calls=%async_computation | async-start | bytes 8388608 | tf_op jit(solution)/shard_map/all_to_all | solution.py:14
  32.0 2.1 gather_fusion.1
  34.2 193.7 %all-to-all-done = bf16[32,128,512]{1,2,0:T(8,128)(2,1)} async-done(((bf16[32,128,512]{1,2,0:T(8,128)(2,1)}), bf16[32,128,512]{1,2,0:T(8,128)(2,1)}, u32[]{:S(2)}, u32[]{:S(2)}) %all-to-all-start) | async-done | bytes 4194336 | tf_op jit(solution)/shard_map/all_to_all | solution.py:14
  227.9 6.9 %copy.48 = bf16[32,128,512]{1,0,2:T(8,128)(2,1)} copy(bf16[32,128,512]{1,2,0:T(8,128)(2,1)} %all-to-all-done) | data formatting | bytes 8388608 | tf_op jit(solution)/shard_map/all_to_all | solution.py:14
  234.8 7.4 %reshape_reshape.3 = bf16[4096,8,64]{0,2,1:T(8,128)(2,1)} reshape(bf16[32,128,512]{1,0,2:T(8,128)(2,1)} %copy.48) | data formatting | bytes 8388608 | tf_op jit(solution)/shard_map/reshape;reshape | solution.py:39
  242.2 40.1 %all-gather.9.cloned.1.call-done = bf16[1,4096,512]{1,2,0:T(8,128)(2,1)} async-done(((bf16[1,128,512]{1,2,0:T(8,128)(2,1)}), bf16[1,4096,512]{1,2,0:T(8,128)(2,1)}) %all-gather.9.cloned.1.call-update) | async-done | bytes 4194320 | tf_op jit(solution)/shard_map/all_gather | solution.py:133
  282.3 29.5 %while.11 = (s32[]{:T(128)}, bf16[8,128,64]{1,2,0:T(8,128)(2,1)S(1)}, bf16[8,128,64]{1,2,0:T(8,128)(2,1)S(1)}, bf16[8,4096,64]{1,2,0:T(8,128)(2,1)}, bf16[8,4096...) while((s32[]{:T(128)}, bf16[8,128,64]{1,2,0:T(8,128)(2,1)S(1)}, ...), condition=%wide.region_3.4_spmd.clone, body=%wide.region_0.3_spmd.clone.sunk | while | flops 138411776 | bytes 7397965 | solution.py:59
  282.3 1.6 fusion.158
  284.4 1.6 fusion.160
  286.0 1.6 fusion.158
  288.0 1.6 fusion.160
  289.7 1.6 fusion.158
  291.7 1.6 fusion.160
  293.4 1.6 fusion.158
  295.4 1.6 fusion.160
  297.0 1.6 fusion.158
  299.1 1.6 fusion.160
  300.7 1.6 fusion.158
  302.8 1.6 fusion.160
  304.4 1.6 fusion.158
  306.4 1.6 fusion.160
  308.1 1.6 fusion.158
  310.1 1.6 fusion.160
  312.6 2.1 gather_fusion
  314.8 42.7 %all-gather.5.cloned.1.call-done = bf16[32,2,128,128]{3,2,1,0:T(8,128)(2,1)} async-done(((bf16[2,2,128,128]{3,2,1,0:T(8,128)(2,1)}), bf16[32,2,128,128]{3,2,1,0:T(8,128)(2,1)}) %all-gather.5.cloned.1.call-update) | async-done | bytes 2097168 | tf_op jit(solution)/shard_map/all_gather | solution.py:144
  357.4 4.3 fusion.32
  361.8 60.9 %all-gather.7.cloned.1.call-done = bf16[32,2,128,128]{3,2,1,0:T(8,128)(2,1)} async-done(((bf16[2,2,128,128]{3,2,1,0:T(8,128)(2,1)}), bf16[32,2,128,128]{3,2,1,0:T(8,128)(2,1)}) %all-gather.7.cloned.1.call-update) | async-done | bytes 2097168 | tf_op jit(solution)/shard_map/all_gather | solution.py:145
  422.6 7.2 %convolution_bitcast_fusion.1 = f32[128,32,2,128]{3,0,2,1:T(8,128)} fusion(bf16[32,2,128,128]{3,2,1,0:T(8,128)(2,1)} %all-gather.5.cloned.1.call-done, f32[32,128,128,1]{2,1,3,0:T(8,128)} %fusion.32, bf16[32,2,128,128]{3,2,1,0:T(8,128)(2,1)} %all-gather.7.cloned.1.call-done, bf16[32,2,128,128]{3,2,1,0:T(8,128)(2,1)} %bitcast.204, pred[32,2]{1,0:T(8,128)(4,1)S(1)} %copy.56), kind=kOutput, calls=%fused_computation.24 | convolution fusion | flops 543162368 | bytes 12582976 | tf_op jit(solution)/shard_map/tcj,cnkj->tcnk/dot_general | solution.py:107
  429.8 6.7 %fusion.96 = (f32[128]{0:T(128)S(1)}, f32[8,128,128,1]{2,0,3,1:T(8,128)S(1)}) fusion(f32[8,128]{1,0:T(8,128)S(1)} %bitcast.211, f32[128,32,2,128]{3,0,2,1:T(8,128)} %convolution_bitcast_fusion.1, s32[32,2]{0,1:T(2,128)S(1)} %copy-done.7), kind=kOutput, calls=%fused_computation.111 | convolution fusion | flops 100925824 | bytes 4723456 | tf_op jit(solution)/shard_map/tcnk,cnb->tbk/dot_general | solution.py:108
  436.8 5.2 %convolution_bitcast_fusion.2 = f32[128,32,2,128]{3,0,2,1:T(8,128)S(1)} fusion(bf16[32,2,128,128]{3,2,1,0:T(8,128)(2,1)S(1)} %copy-done.9, f32[32,128,128,1]{2,1,3,0:T(8,128)S(1)} %copy-done.1), kind=kOutput, calls=%fused_computation.25 | convolution fusion | flops 302514176 | bytes 8388608 | tf_op jit(solution)/shard_map/tck,cnkj->tcnj/dot_general | solution.py:98
  441.9 3.8 fusion.15
  (64 shorter events, 10.3 us)
Async XLA Ops:
  7.2 304.6 %copy-start = (bf16[512,1024]{1,0:T(8,128)(2,1)S(1)}, bf16[512,1024]{1,0:T(8,128)(2,1)}, u32[]{:S(2)}) copy-start(bf16[512,1024]{1,0:T(8,128)(2,1)} %param.21) | copy-start | bytes 3145732
  11.2 17.3 %copy-start.4 = (bf16[1,128,512]{2,1,0:T(8,128)(2,1)S(1)}, bf16[1,128,512]{2,1,0:T(8,128)(2,1)}, u32[]{:S(2)}) copy-start(bf16[1,128,512]{2,1,0:T(8,128)(2,1)} %param.18) | copy-start | bytes 393220
  11.2 19.6 %copy-start.5 = (bf16[1,128,512]{2,1,0:T(8,128)(2,1)S(1)}, bf16[1,128,512]{2,1,0:T(8,128)(2,1)}, u32[]{:S(2)}) copy-start(bf16[1,128,512]{2,1,0:T(8,128)(2,1)} %param.17) | copy-start | bytes 393220
  11.2 19.7 %copy-start.7 = (s32[32,2]{0,1:T(2,128)S(1)}, s32[32,2]{0,1:T(2,128)}, u32[]{:S(2)}) copy-start(s32[32,2]{0,1:T(2,128)} %param.24) | copy-start | bytes 772
  11.2 20.1 %copy-start.2 = (bf16[1,128,1024]{2,1,0:T(8,128)(2,1)S(1)}, bf16[1,128,1024]{2,1,0:T(8,128)(2,1)}, u32[]{:S(2)}) copy-start(bf16[1,128,1024]{2,1,0:T(8,128)(2,1)} %param.27) | copy-start | bytes 786436
  11.2 20.4 %copy-start.8 = (s32[32,2]{0,1:T(2,128)S(1)}, s32[32,2]{0,1:T(2,128)}, u32[]{:S(2)}) copy-start(s32[32,2]{0,1:T(2,128)} %param.26) | copy-start | bytes 772
  11.2 216.7 %all-to-all-start = ((bf16[32,128,512]{1,2,0:T(8,128)(2,1)}), bf16[32,128,512]{1,2,0:T(8,128)(2,1)}, u32[]{:S(2)}, u32[]{:S(2)}) async-start(bf16[32,128,512]{1,2,0:T(8,128)(2,1)} %stack.3), calls=%async_computation | async-start | bytes 8388608 | tf_op jit(solution)/shard_map/all_to_all | solution.py:14
  28.5 253.8 %all-gather.9.cloned.1.call-start = ((), (), s32[]{:S(2)}) async-start(), calls=%async_computation.3 | async-start | bytes 4325376 | tf_op jit(solution)/shard_map/all_gather | solution.py:133
  29.3 328.1 %all-gather.5.cloned.1.call-start = ((), (), s32[]{:S(2)}) async-start(), calls=%async_computation.1 | async-start | bytes 2228224 | tf_op jit(solution)/shard_map/all_gather | solution.py:144
  30.1 392.6 %all-gather.7.cloned.1.call-start = ((), (), s32[]{:S(2)}) async-start(), calls=%async_computation.2 | async-start | bytes 2228224 | tf_op jit(solution)/shard_map/all_gather | solution.py:145
  32.0 2.2 copy-start.10
  282.3 29.5 %copy-start.3 = (bf16[1,128,1024]{2,1,0:T(8,128)(2,1)S(1)}, bf16[1,128,1024]{2,1,0:T(8,128)(2,1)}, u32[]{:S(2)}) copy-start(bf16[1,128,1024]{2,1,0:T(8,128)(2,1)} %param.16) | copy-start | bytes 786436
  311.8 0.7 copy-start.6
  429.8 7.0 %copy-start.1 = (f32[32,128,128,1]{2,1,3,0:T(8,128)S(1)}, f32[32,128,128,1]{2,1,3,0:T(8,128)}, u32[]{:S(2)}) copy-start(f32[32,128,128,1]{2,1,3,0:T(8,128)} %fusion.32) | copy-start | bytes 6291460
  429.8 7.0 %copy-start.9 = (bf16[32,2,128,128]{3,2,1,0:T(8,128)(2,1)S(1)}, bf16[32,2,128,128]{3,2,1,0:T(8,128)(2,1)}, u32[]{:S(2)}) copy-start(bf16[32,2,128,128]{3,2,1,0:T(8,128)(2,1)} %all-gather.7.cloned.1.call-done) | copy-start | bytes 6291460
Sparse Core Ops, SparseCore 0:
  31.9 250.3 all-gather.8
  285.6 71.7 all-gather.4
  360.8 61.7 all-gather.6
